TPU v7x, 32 devices: a whole 2x2x4 slice. The times are simulated.
32 devices in a mesh: row: 8 (over y, x, core), col: 4 (over z).
Axes of the slice: x: 2, y: 2, z: 4, core: 2. Of those that a mesh axis runs over, the one named last changes fastest.
Arguments:
- pooled: bfloat16 [4096, 1152], P(('row', 'col')), may hold values from -6 to 6
- text_embed: bfloat16 [4096, 1152], P(('row', 'col')), may hold values from -0.29882812 to 0.29882812
- head_weight: bfloat16 [1152, 1152], replicated, may hold values from -0.1875 to 0.1875
- logit_scale: float32 [4], replicated, may hold values from 1 to 4
- logit_bias: float32 [4], replicated, may hold values from -2 to 0
- partner: int32 [32, 128], P(('row', 'col')), may hold values from 0 to 127, each once within a row
Outputs:
- text_grad: float32 [4096, 1152], P(('row', 'col'))
- head_grad: float32 [1152, 1152], P('row', 'col')
Inputs may be any that keep to these rules, and one draw needn't show every extreme that they name: Each row of partner is a permutation of the indices within a block.
All inputs are finite; a program needn't handle non-finite values.
Results may differ from a plain program's by a relative error of at most 0.004.
Values may be sent and summed in bfloat16 or wider, within the bound.
A program may use at most 64 MiB of HBM per device.

v0:
```python
import math

import jax
import jax.numpy as jnp
from jax import lax
from jax.sharding import PartitionSpec as P


def shifted(value, axis, by):
    count = lax.axis_size(axis)
    return lax.ppermute(value, axis, [(i, (i + by) % count) for i in range(count)])


def segment_weights(image_part, text_part, positive, logit_scale, logit_bias, factor):
    model_width = image_part.shape[1]
    bounds = [0, model_width // 8, model_width // 4, model_width // 2, model_width]
    running = jnp.zeros((image_part.shape[0], text_part.shape[0]), jnp.float32)
    level_grads = []
    for prefix in range(4):
        low_end = bounds[prefix]
        high_end = bounds[prefix + 1]
        running = running + jnp.dot(
            image_part[:, low_end:high_end],
            text_part[:, low_end:high_end].T,
            preferred_element_type=jnp.float32,
        )
        logits = logit_scale[prefix] * running + logit_bias[prefix]
        level_grads.append((jax.nn.sigmoid(logits) - positive) * factor)
    weights = []
    carried = jnp.zeros_like(running)
    for prefix in range(3, -1, -1):
        carried = carried + logit_scale[prefix] * level_grads[prefix]
        weights.insert(0, carried.astype(jnp.bfloat16))
    return (weights, bounds)


def image_side(weights, bounds, text_part):
    pieces = []
    for prefix in range(4):
        pieces.append(
            jnp.dot(
                weights[prefix],
                text_part[:, bounds[prefix] : bounds[prefix + 1]],
                preferred_element_type=jnp.float32,
            )
        )
    return jnp.concatenate(pieces, 1)


def text_side(weights, bounds, image_part):
    pieces = []
    for prefix in range(4):
        pieces.append(
            jnp.dot(
                weights[prefix].T,
                image_part[:, bounds[prefix] : bounds[prefix + 1]],
                preferred_element_type=jnp.float32,
            )
        )
    return jnp.concatenate(pieces, 1)


def body(pooled, text_embed, head_weight, logit_scale, logit_bias, partner):
    block_rows = pooled.shape[0]
    factor = 1.0 / math.sqrt(block_rows * lax.axis_size("row") * lax.axis_size("col"))
    embedding = jnp.dot(pooled, head_weight, preferred_element_type=jnp.float32).astype(
        jnp.bfloat16
    )
    local_ids = jnp.arange(block_rows, dtype=jnp.int32)
    positive = (partner[0][:, None] == local_ids[None, :]).astype(jnp.float32)
    empty = jnp.zeros((block_rows, block_rows), jnp.float32)
    weights, bounds = segment_weights(
        embedding, text_embed, positive, logit_scale, logit_bias, factor
    )
    own_image = image_side(weights, bounds, text_embed)
    own_text = text_side(weights, bounds, embedding)
    behind = shifted(text_embed, "row", 1)
    weights, bounds = segment_weights(embedding, behind, empty, logit_scale, logit_bias, factor)
    cross_image = image_side(weights, bounds, behind)
    cross_text = text_side(weights, bounds, embedding)
    returned = shifted(cross_text.astype(jnp.bfloat16), "row", -1).astype(cross_text.dtype)
    text_grad = own_text + returned
    image_grad = own_image + cross_image
    column_block = lax.all_to_all(
        image_grad.astype(jnp.bfloat16), "col", split_axis=1, concat_axis=0, tiled=True
    ).astype(image_grad.dtype)
    group_rows = lax.all_gather(pooled, "col", axis=0, tiled=True)
    block_term = jnp.dot(
        group_rows.astype(jnp.float32).T, column_block, precision=lax.Precision.HIGHEST
    )
    head_grad = lax.psum_scatter(block_term, "row", scatter_dimension=0, tiled=True)
    return (text_grad, head_grad)


def solution(mesh):
    in_specs = (
        P(("row", "col"), None),
        P(("row", "col"), None),
        P(),
        P(),
        P(),
        P(("row", "col"), None),
    )
    out_specs = (P(("row", "col"), None), P("row", "col"))
    return jax.shard_map(body, mesh=mesh, in_specs=in_specs, out_specs=out_specs, check_vma=False)
```

profile of v0, /device:TPU:0, one launch (start us, length us, event | category | flops | bytes accessed | tf_op | source)
XLA Modules:
  0.0 100.0 jit_solution(16892916511603823960)
XLA Ops:
  7.2 0.0 copy-start
  7.2 0.0 all-gather.2.cloned.1.call-start
  7.2 0.5 collective-permute-start
  7.8 0.1 all-gather.2.cloned.1.call-update
  7.9 1.0 %copy-done = bf16[1152,1152]{1,0:T(8,128)(2,1)S(1)} copy-done((bf16[1152,1152]{1,0:T(8,128)(2,1)S(1)}, bf16[1152,1152]{1,0:T(8,128)(2,1)}, u32[]{:S(2)}) %copy-start) | copy-done | bytes 2654232
  8.9 1.6 %convolution_convert_fusion = bf16[128,1152]{1,0:T(8,128)(2,1)S(1)} fusion(bf16[128,1152]{1,0:T(8,128)(2,1)} %param.6, bf16[1152,1152]{1,0:T(8,128)(2,1)S(1)} %copy-done), kind=kOutput, calls=%fused_computation.1 | convolution fusion | flops 339886080 | bytes 3244032 | tf_op jit(solution)/shard_map/dot_general | solution.py:66
  10.5 0.7 fusion.86
  13.8 0.7 fusion.85
  14.5 0.2 fusion.59
  14.6 0.2 convolution_add_fusion.3
  14.9 0.3 convolution_add_fusion.2
  15.2 5.4 %fusion.41 = (bf16[128,128]{1,0:T(8,128)(2,1)S(1)}, bf16[128,128]{1,0:T(8,128)(2,1)S(1)}, bf16[128,128]{1,0:T(8,128)(2,1)S(1)}, bf16[128,128]{1,0:T(8,128)(2,1)S(1)}) fusion(f32[128,128]{1,0:T(8,128)S(1)} %fusion.59, f32[]{:T(128)S(6)} %mul.113, f32[]{:T(128)} %bitcast.8, f32[]{:T(128)} %bitcast.7, s32[128]{0:T(128)S(1)} %bitcast.40, f32[]{:T(128)S(6)} %mul.108, ...), kind=kOutput, calls=%fused_computation.59 | convolution fusion | flops 19496960 | bytes 655920 | tf_op jit(solution)/shard_map/dot_general | solution.py:22
  20.6 0.0 copy-start.6
  20.6 0.0 copy-start.8
  20.6 0.0 copy-start.4
  20.6 0.3 fusion.32
  20.9 0.3 fusion.54
  21.2 0.2 fusion.57
  21.4 0.3 fusion.21
  21.8 0.0 collective-permute-done
  21.8 0.1 fusion.52
  22.0 0.3 convolution_add_fusion.1
  22.2 0.3 convolution_add_fusion
  22.5 5.4 %add_convert_fusion = (bf16[128,128]{1,0:T(8,128)(2,1)S(1)}, bf16[128,128]{1,0:T(8,128)(2,1)S(1)}, bf16[128,128]{1,0:T(8,128)(2,1)S(1)}, bf16[128,128]{1,0:T(8,128)(2,1)S(1)}) fusion(f32[128,128]{1,0:T(8,128)S(1)} %fusion.52, f32[]{:T(128)S(6)} %mul.113, f32[]{:T(128)} %bitcast.8, f32[]{:T(128)} %bitcast.7, f32[]{:T(128)S(6)} %mul.108, f32[]{:T(128)} %bitcast.6, ...), kind=kOutput, calls=%fused_computation.60 | convolution fusion | flops 19398656 | bytes 655408 | tf_op jit(solution)/shard_map/dot_general | solution.py:22
  28.0 0.3 fusion.47
  28.3 0.2 fusion.50
  28.5 0.3 fusion.29
  28.8 0.0 copy-start.5
  28.8 0.3 fusion.18
  29.1 0.8 fusion.15
  29.9 6.3 %all-to-all-start = ((bf16[128,4,288]{0,2,1:T(8,128)(2,1)}), bf16[128,4,288]{0,2,1:T(8,128)(2,1)S(1)}, u32[]{:S(2)}, u32[]{:S(2)}) async-start(bf16[128,4,288]{0,2,1:T(8,128)(2,1)} %bitcast.9), calls=%async_computation | async-start | bytes 589824 | tf_op jit(solution)/shard_map/all_to_all | solution.py:84
  36.3 0.9 fusion.63
  37.2 0.9 fusion.44
  38.1 10.8 %all-to-all-done = bf16[128,4,288]{0,2,1:T(8,128)(2,1)S(1)} async-done(((bf16[128,4,288]{0,2,1:T(8,128)(2,1)}), bf16[128,4,288]{0,2,1:T(8,128)(2,1)S(1)}, u32[]{:S(2)}, u32[]{:S(2)}) %all-to-all-start) | async-done | bytes 294944 | tf_op jit(solution)/shard_map/all_to_all | solution.py:84
  48.9 2.9 %convolution_bitcast_fusion = f32[1152,288]{0,1:T(8,128)} fusion(bf16[512,1152]{1,0:T(8,128)(2,1)} %all-gather.2.cloned.1.call-done, bf16[128,4,288]{0,2,1:T(8,128)(2,1)S(1)} %all-to-all-done), kind=kOutput, calls=%fused_computation | convolution fusion | flops 339738624 | bytes 2801664 | tf_op jit(solution)/shard_map/dot_general | solution.py:88
  51.8 3.1 %copy.16 = f32[1152,288]{1,0:T(8,128)} copy(f32[1152,288]{0,1:T(8,128)} %convolution_bitcast_fusion) | data formatting | bytes 2654208
  54.9 0.0 reduce-scatter.4.cloned.1.call-update
  54.9 0.2 convolution_convert_fusion.4
  55.1 0.3 convolution_convert_fusion.3
  55.4 0.3 convolution_convert_fusion.2
  55.7 0.3 convolution_convert_fusion.1
  56.1 2.0 %collective-permute-start.1 = (bf16[128,1152]{0,1:T(8,128)(2,1)S(1)}, bf16[128,1152]{0,1:T(8,128)(2,1)S(1)}, u32[]{:S(2)}, u32[]{:S(2)}) collective-permute-start(bf16[128,1152]{0,1:T(8,128)(2,1)S(1)} %pad_maximum_fusion), channel_id=1, source_target_pairs={{0,28},{4,0},{8,4},{12,8},{16,12},{20,16},{24,20},{28,24},{1,29},{... | collective-permute-start | bytes 884744 | tf_op jit(solution)/shard_map/ppermute | solution.py:11
  58.1 0.2 fusion.68
  58.3 0.3 fusion.26
  58.6 3.7 %collective-permute-done.1 = bf16[128,1152]{0,1:T(8,128)(2,1)S(1)} collective-permute-done((bf16[128,1152]{0,1:T(8,128)(2,1)S(1)}, bf16[128,1152]{0,1:T(8,128)(2,1)S(1)}, u32[]{:S(2)}, u32[]{:S(2)}) %collective-permute-start.1) | collective-permute-done | bytes 294944 | tf_op jit(solution)/shard_map/ppermute | solution.py:11
  62.3 0.1 maximum_add_fusion
  62.4 1.1 %copy.14 = f32[128,1152]{1,0:T(8,128)} copy(f32[128,1152]{0,1:T(8,128)S(1)} %maximum_add_fusion) | data formatting | bytes 1179648
  63.4 29.7 %reduce-scatter.4.cloned.1.call-done = f32[144,288]{1,0:T(8,128)} async-done(((f32[1152,288]{1,0:T(8,128)}), f32[144,288]{1,0:T(8,128)}) %reduce-scatter.4.cloned.1.call-update) | async-done | bytes 165904
  (27 shorter events, 0.1 us)
Async XLA Ops:
  7.2 1.8 %copy-start = (bf16[1152,1152]{1,0:T(8,128)(2,1)S(1)}, bf16[1152,1152]{1,0:T(8,128)(2,1)}, u32[]{:S(2)}) copy-start(bf16[1152,1152]{1,0:T(8,128)(2,1)} %param.8) | copy-start | bytes 7962628
  7.2 41.7 %all-gather.2.cloned.1.call-start = ((), (), s32[]{:S(2)}) async-start(), calls=%async_computation.2 | async-start | bytes 1474560 | tf_op jit(solution)/shard_map/all_gather | solution.py:87
  7.2 14.6 %collective-permute-start = (bf16[128,1152]{1,0:T(8,128)(2,1)}, bf16[128,1152]{1,0:T(8,128)(2,1)S(1)}, u32[]{:S(2)}, u32[]{:S(2)}) collective-permute-start(bf16[128,1152]{1,0:T(8,128)(2,1)} %param.7), channel_id=1, source_target_pairs={{0,4},{4,8},{8,12},{12,16},{16,20},{20,24},{24,28},{28,0},{1,5},{5... | collective-permute-start | bytes 884744 | tf_op jit(solution)/shard_map/ppermute | solution.py:11
  8.9 1.6 %copy-start.12 = (f32[4]{0:T(128)S(1)}, f32[4]{0:T(128)}, u32[]{:S(2)}) copy-start(f32[4]{0:T(128)} %param.9) | copy-start | bytes 52
  8.9 4.9 %copy-start.13 = (f32[4]{0:T(128)S(1)}, f32[4]{0:T(128)}, u32[]{:S(2)}) copy-start(f32[4]{0:T(128)} %param.10) | copy-start | bytes 52
  8.9 5.5 %copy-start.1 = (bf16[128,1152]{1,0:T(8,128)(2,1)S(1)}, bf16[128,1152]{1,0:T(8,128)(2,1)}, u32[]{:S(2)}) copy-start(bf16[128,1152]{1,0:T(8,128)(2,1)} %param.7) | copy-start | bytes 884740
  8.9 6.2 %copy-start.14 = (s32[1,128]{1,0:T(1,128)S(1)}, s32[1,128]{1,0:T(1,128)}, u32[]{:S(2)}) copy-start(s32[1,128]{1,0:T(1,128)} %param.11) | copy-start | bytes 1540
  20.6 1.2 %copy-start.6 = (bf16[128,128]{1,0:T(8,128)(2,1)}, bf16[128,128]{1,0:T(8,128)(2,1)S(1)}, u32[]{:S(2)}) copy-start(bf16[128,128]{1,0:T(8,128)(2,1)S(1)} %get-tuple-element.11) | copy-start | bytes 98308
  20.6 1.2 %copy-start.8 = (bf16[128,128]{1,0:T(8,128)(2,1)}, bf16[128,128]{1,0:T(8,128)(2,1)S(1)}, u32[]{:S(2)}) copy-start(bf16[128,128]{1,0:T(8,128)(2,1)S(1)} %get-tuple-element.12) | copy-start | bytes 98308
  20.6 1.2 %copy-start.10 = (bf16[128,128]{1,0:T(8,128)(2,1)}, bf16[128,128]{1,0:T(8,128)(2,1)S(1)}, u32[]{:S(2)}) copy-start(bf16[128,128]{1,0:T(8,128)(2,1)S(1)} %get-tuple-element.22) | copy-start | bytes 98308
  20.6 7.3 %copy-start.4 = (bf16[128,128]{1,0:T(8,128)(2,1)}, bf16[128,128]{1,0:T(8,128)(2,1)S(1)}, u32[]{:S(2)}) copy-start(bf16[128,128]{1,0:T(8,128)(2,1)S(1)} %get-tuple-element.13) | copy-start | bytes 98308
  28.8 7.5 %copy-start.9 = (bf16[128,128]{1,0:T(8,128)(2,1)S(1)}, bf16[128,128]{1,0:T(8,128)(2,1)}, u32[]{:S(2)}) copy-start(bf16[128,128]{1,0:T(8,128)(2,1)} %copy-done.8) | copy-start | bytes 98308
  28.8 8.4 %copy-start.5 = (bf16[128,128]{1,0:T(8,128)(2,1)S(1)}, bf16[128,128]{1,0:T(8,128)(2,1)}, u32[]{:S(2)}) copy-start(bf16[128,128]{1,0:T(8,128)(2,1)} %copy-done.4) | copy-start | bytes 98308
  29.9 19.0 %all-to-all-start = ((bf16[128,4,288]{0,2,1:T(8,128)(2,1)}), bf16[128,4,288]{0,2,1:T(8,128)(2,1)S(1)}, u32[]{:S(2)}, u32[]{:S(2)}) async-start(bf16[128,4,288]{0,2,1:T(8,128)(2,1)} %bitcast.9), calls=%async_computation | async-start | bytes 589824 | tf_op jit(solution)/shard_map/all_to_all | solution.py:84
  36.3 56.9 %reduce-scatter.4.cloned.1.call-start = ((), (), s32[]{:S(2)}) async-start(), calls=%async_computation.3 | async-start | bytes 1990656
  54.9 3.2 %copy-start.7 = (bf16[128,128]{1,0:T(8,128)(2,1)S(1)}, bf16[128,128]{1,0:T(8,128)(2,1)}, u32[]{:S(2)}) copy-start(bf16[128,128]{1,0:T(8,128)(2,1)} %copy-done.6) | copy-start | bytes 98308
  54.9 3.4 %copy-start.11 = (bf16[128,128]{1,0:T(8,128)(2,1)S(1)}, bf16[128,128]{1,0:T(8,128)(2,1)}, u32[]{:S(2)}) copy-start(bf16[128,128]{1,0:T(8,128)(2,1)} %copy-done.10) | copy-start | bytes 98308
  54.9 7.4 %copy-start.2 = (f32[128,288]{0,1:T(8,128)S(1)}, f32[128,288]{0,1:T(8,128)}, u32[]{:S(2)}) copy-start(f32[128,288]{0,1:T(8,128)} %fusion.44) | copy-start | bytes 442372
  54.9 7.4 %copy-start.3 = (f32[128,144]{0,1:T(8,128)S(1)}, f32[128,144]{0,1:T(8,128)}, u32[]{:S(2)}) copy-start(f32[128,144]{0,1:T(8,128)} %fusion.63) | copy-start | bytes 221188
  56.1 6.2 %collective-permute-start.1 = (bf16[128,1152]{0,1:T(8,128)(2,1)S(1)}, bf16[128,1152]{0,1:T(8,128)(2,1)S(1)}, u32[]{:S(2)}, u32[]{:S(2)}) collective-permute-start(bf16[128,1152]{0,1:T(8,128)(2,1)S(1)} %pad_maximum_fusion), channel_id=1, source_target_pairs={{0,28},{4,0},{8,4},{12,8},{16,12},{20,16},{24,20},{28,24},{1,29},{... | collective-permute-start | bytes 884744 | tf_op jit(solution)/shard_map/ppermute | solution.py:11
Sparse Core Ops, SparseCore 0:
  9.6 36.1 all-gather.1
  55.0 38.0 reduce-scatter.3
where the time goes:
time: 101 us; the launch traced here: 100 us
  waiting for transfers between devices  44.3 us (44%)
  matrix products  22.5 us (22%)
  between operations  16.9 us (17%)
  starting transfers between devices  8.91 us (9%)
  local copies, waits for them, and re-layouts  6.56 us (6%)
    unnamed x3, waiting for transfers between devices  29.9 us
    dot_general x8, matrix products, segment_weights(): jnp.dot(image_part[:, low_end:high_end], text_part[:, low_end:high_end].T...  12.2 us
    all_to_all x1, waiting for transfers between devices, body(): lax.all_to_all(image_grad.astype(jnp.bfloat16), 'col', split_axis=1, conc...  10.8 us
    all_to_all x1, starting transfers between devices, body(): lax.all_to_all(image_grad.astype(jnp.bfloat16), 'col', split_axis=1, conc...  6.35 us
    unnamed x32, local copies, waits for them, and re-layouts  5.24 us
    ppermute x2, waiting for transfers between devices, shifted(): lax.ppermute(value, axis, [(i, (i + by) % count) for i in range(count)])  3.68 us
    dot_general x8, matrix products, text_side(): jnp.dot(weights[prefix].T, image_part[:, bounds[prefix]:bounds[prefix + 1...  3.52 us
    dot_general x1, matrix products, body(): jnp.dot(group_rows.astype(jnp.float32).T, column_block, precision=lax.Pre...  2.88 us
  transfers between devices with their start and end apart: 5, of which 3 were waited for; matrix products, arithmetic and copies ran while one was open for 23% of the time, Pallas kernels for 0%

commit v1 on v0

--- a/solution.py
+++ b/solution.py
@@ -1,9 +1,15 @@
+import functools
 import math
 
 import jax
 import jax.numpy as jnp
 from jax import lax
+from jax.experimental import pallas as pl
+from jax.experimental.pallas import tpu as pltpu
 from jax.sharding import PartitionSpec as P
+
+LANES = 128
+MESH = pl.DeviceIdType.MESH
 
 
 def shifted(value, axis, by):
@@ -92,6 +98,387 @@
     return (text_grad, head_grad)
 
 
+def dot_nt(left, right):
+    return lax.dot_general(
+        left, right, (((1,), (1,)), ((), ())), preferred_element_type=jnp.float32
+    )
+
+
+def dot_nn(left, right):
+    return jnp.dot(left, right, preferred_element_type=jnp.float32)
+
+
+def aligned(low_end, high_end):
+    return low_end // LANES * LANES, -(-high_end // LANES) * LANES
+
+
+def weights_of(score_of, positive, scale_ref, bias_ref, factor):
+    running = None
+    level_grads = []
+    for prefix in range(4):
+        part = score_of(prefix)
+        running = part if running is None else running + part
+        gate = jax.nn.sigmoid(scale_ref[prefix] * running + bias_ref[prefix])
+        if positive is not None:
+            gate = gate - positive
+        level_grads.append(gate * factor)
+    weights = [None] * 4
+    carried = None
+    for prefix in range(3, -1, -1):
+        term = scale_ref[prefix] * level_grads[prefix]
+        carried = term if carried is None else carried + term
+        weights[prefix] = carried.astype(jnp.bfloat16)
+    return weights
+
+
+def by_tile(piece_of, bounds, store):
+    pieces = []
+    for q in range(4):
+        start, stop = aligned(bounds[q], bounds[q + 1])
+        pieces.append((start, stop, piece_of(q, start, stop)))
+    for tile in range(bounds[4] // LANES):
+        base = tile * LANES
+        value = None
+        for q in range(4):
+            start, stop, piece = pieces[q]
+            if start <= base < stop:
+                here = piece[:, base - start : base - start + LANES]
+                if value is None:
+                    value = here
+                else:
+                    lane = lax.broadcasted_iota(jnp.int32, here.shape, 1)
+                    value = jnp.where(lane < bounds[q] - base, value, here)
+        store(base, value)
+
+
+def kernel(
+    n_row,
+    n_col,
+    factor,
+    pooled_ref,
+    text_ref,
+    weight_ref,
+    scale_ref,
+    bias_ref,
+    partner_ref,
+    text_grad_ref,
+    head_grad_ref,
+    pooled_ahead,
+    text_behind,
+    pooled_t,
+    pooled_cols,
+    embed,
+    masked,
+    image,
+    total,
+    sent,
+    landed,
+    near_send,
+    near_recv,
+    pool_send,
+    pool_recv,
+    image_send,
+    image_recv,
+    out_send,
+    out_recv,
+):
+    rows, width = pooled_ref.shape
+    chips = n_row // 2
+    head_rows = width // n_row
+    head_cols = width // n_col
+    window = landed.shape[2]
+    bounds = [0, width // 8, width // 4, width // 2, width]
+    row = lax.axis_index("row")
+    col = lax.axis_index("col")
+    chip = row // 2
+    core = row % 2
+
+    def peer(k, e):
+        other = core if e == 0 else 1 - core
+        return ((chip + k) % chips) * 2 + other
+
+    barrier = pltpu.get_barrier_semaphore()
+    for d in range(1, n_row):
+        pl.semaphore_signal(
+            barrier, inc=1, device_id=((row + d) % n_row, col), device_id_type=MESH
+        )
+    for d in range(1, n_col):
+        pl.semaphore_signal(
+            barrier, inc=1, device_id=(row, (col + d) % n_col), device_id_type=MESH
+        )
+
+    def remote(src, dst, send, recv, device):
+        return pltpu.make_async_remote_copy(
+            src_ref=src,
+            dst_ref=dst,
+            send_sem=send,
+            recv_sem=recv,
+            device_id=device,
+            device_id_type=MESH,
+        )
+
+    behind_copy = remote(
+        text_ref, text_behind, near_send.at[0], near_recv.at[0], ((row + 1) % n_row, col)
+    )
+    ahead_copy = remote(
+        pooled_ref,
+        pooled_ahead,
+        near_send.at[1],
+        near_recv.at[1],
+        ((row + n_row - 1) % n_row, col),
+    )
+    pl.semaphore_wait(barrier, n_row + n_col - 2)
+    behind_copy.start()
+    ahead_copy.start()
+
+    for tile in range(width // LANES):
+        lanes = pl.ds(tile * LANES, LANES)
+        pooled_t[lanes, :] = pooled_ref[:, lanes].T
+    pool_copies = []
+    for k in range(chips):
+        for e in range(2):
+            slot = 2 * k + e
+            if slot == 0:
+                continue
+            target = peer(k, e)
+            copy = remote(
+                pooled_t.at[pl.ds(pl.multiple_of(target * head_rows, 16), head_rows), :],
+                pooled_cols.at[:, pl.ds(slot * rows, rows)],
+                pool_send.at[slot],
+                pool_recv.at[slot],
+                (target, col),
+            )
+            copy.start()
+            pool_copies.append(copy)
+    pooled_cols[:, pl.ds(0, rows)] = pooled_t[
+        pl.ds(pl.multiple_of(row * head_rows, 16), head_rows), :
+    ]
+
+    def fill_embed(source):
+        at = 0
+        for q in range(4):
+            start, stop = aligned(bounds[q], bounds[q + 1])
+            at += stop - start
+        step = 3 * LANES if width % (3 * LANES) == 0 else LANES
+        for base in range(0, width, step):
+            part = dot_nn(source[...], weight_ref[:, pl.ds(base, step)])
+            embed[:, pl.ds(base, step)] = part.astype(jnp.bfloat16)
+        at = 0
+        for q in range(4):
+            start, stop = aligned(bounds[q], bounds[q + 1])
+            part = embed[:, pl.ds(start, stop - start)].astype(jnp.float32)
+            lane = lax.broadcasted_iota(jnp.int32, part.shape, 1) + start
+            keep = (lane >= bounds[q]) & (lane < bounds[q + 1])
+            masked[:, pl.ds(at, stop - start)] = jnp.where(keep, part, 0.0).astype(
+                jnp.bfloat16
+            )
+            at += stop - start
+
+    def masked_part(q):
+        at = 0
+        for before in range(q):
+            start, stop = aligned(bounds[before], bounds[before + 1])
+            at += stop - start
+        start, stop = aligned(bounds[q], bounds[q + 1])
+        return masked[:, pl.ds(at, stop - start)]
+
+    def text_part(ref, q):
+        start, stop = aligned(bounds[q], bounds[q + 1])
+        return ref[:, pl.ds(start, stop - start)]
+
+    fill_embed(pooled_ref)
+    text_id = lax.broadcasted_iota(jnp.int32, (rows, rows), 0)
+    positive = (text_id == partner_ref[...]).astype(jnp.float32).T
+    own = weights_of(
+        lambda q: dot_nt(masked_part(q), text_part(text_ref, q)),
+        positive,
+        scale_ref,
+        bias_ref,
+        factor,
+    )
+    behind_copy.wait_recv()
+    cross = weights_of(
+        lambda q: dot_nt(masked_part(q), text_part(text_behind, q)),
+        None,
+        scale_ref,
+        bias_ref,
+        factor,
+    )
+
+    def image_piece(q, start, stop):
+        lanes = pl.ds(start, stop - start)
+        return dot_nn(own[q], text_ref[:, lanes]) + dot_nn(cross[q], text_behind[:, lanes])
+
+    def store_image(base, value):
+        image[pl.ds(0, rows), pl.ds(base, LANES)] = value.astype(jnp.bfloat16)
+
+    by_tile(image_piece, bounds, store_image)
+
+    def slot_rows(slot):
+        return image.at[pl.ds(slot * rows, rows), :]
+
+    image_copies = {}
+    for slot in [1] + [2 * k for k in range(1, chips)]:
+        image_copies[slot] = remote(
+            slot_rows(0),
+            slot_rows(slot),
+            image_send.at[slot],
+            image_recv.at[slot],
+            (peer(slot // 2, slot % 2), col),
+        )
+        image_copies[slot].start()
+
+    def own_text_piece(q, start, stop):
+        return dot_nn(own[q].T, embed[:, pl.ds(start, stop - start)])
+
+    def store_text(base, value):
+        text_grad_ref[:, pl.ds(base, LANES)] = value
+
+    by_tile(own_text_piece, bounds, store_text)
+
+    ahead_copy.wait_recv()
+    fill_embed(pooled_ahead)
+    ahead = weights_of(
+        lambda q: dot_nt(text_part(text_ref, q), masked_part(q)),
+        None,
+        scale_ref,
+        bias_ref,
+        factor,
+    )
+
+    def ahead_piece(q, start, stop):
+        return dot_nn(ahead[q], embed[:, pl.ds(start, stop - start)])
+
+    def add_text(base, value):
+        lanes = pl.ds(base, LANES)
+        text_grad_ref[:, lanes] = text_grad_ref[:, lanes] + value
+
+    by_tile(ahead_piece, bounds, add_text)
+
+    for k in range(1, chips):
+        slot = 2 * k
+        image_copies[slot].wait_recv()
+        image_copies[slot + 1] = remote(
+            slot_rows(slot),
+            slot_rows(slot + 1),
+            image_send.at[slot + 1],
+            image_recv.at[slot + 1],
+            (peer(0, 1), col),
+        )
+        image_copies[slot + 1].start()
+    for copy in pool_copies:
+        copy.wait_recv()
+    image_copies[1].wait_recv()
+    for k in range(1, chips):
+        image_copies[2 * k + 1].wait_recv()
+    step = 3 * LANES if width % (3 * LANES) == 0 else LANES
+    for base in range(0, width, step):
+        lanes = pl.ds(base, step)
+        part = dot_nn(pooled_cols[...], image[:, lanes])
+        total[:, lanes] = part
+        sent[:, lanes] = part.astype(jnp.bfloat16)
+
+    def out_copy(d):
+        target = (col + d) % n_col
+        first = pl.multiple_of(target * head_cols // LANES * LANES, LANES)
+        return remote(
+            sent.at[:, pl.ds(first, window)],
+            landed.at[d - 1],
+            out_send.at[d - 1],
+            out_recv.at[d - 1],
+            (row, target),
+        )
+
+    out_copies = [out_copy(d) for d in range(n_col - 1, 0, -1)]
+    for copy in out_copies:
+        copy.start()
+    mine = col * head_cols // LANES * LANES
+    result = total[:, pl.ds(pl.multiple_of(mine, LANES), window)]
+    for d in range(1, n_col):
+        out_copies[n_col - 1 - d].wait_recv()
+        result = result + landed[d - 1].astype(jnp.float32)
+    offset = col * head_cols - mine
+    head_grad_ref[...] = pltpu.roll(result, (window - offset) % window, 1)[:, :head_cols]
+
+    behind_copy.wait_send()
+    ahead_copy.wait_send()
+    for copy in pool_copies:
+        copy.wait_send()
+    for slot in sorted(image_copies):
+        image_copies[slot].wait_send()
+    for copy in out_copies:
+        copy.wait_send()
+
+
+def window_of(width, n_col):
+    head_cols = width // n_col
+    spans = [aligned(c * head_cols, (c + 1) * head_cols) for c in range(n_col)]
+    window = max(stop - start for start, stop in spans)
+    fits = all(start + window <= width for start, _ in spans)
+    return window, fits
+
+
+def fused_body(n_row, n_col, pooled, text_embed, head_weight, logit_scale, logit_bias, partner):
+    rows, width = pooled.shape
+    factor = 1.0 / math.sqrt(rows * n_row * n_col)
+    window, _ = window_of(width, n_col)
+    bounds = [0, width // 8, width // 4, width // 2, width]
+    spans = [aligned(bounds[q], bounds[q + 1]) for q in range(4)]
+    masked_width = sum(stop - start for start, stop in spans)
+    head_rows, head_cols = width // n_row, width // n_col
+    vmem = pl.BlockSpec(memory_space=pltpu.VMEM)
+    smem = pl.BlockSpec(memory_space=pltpu.SMEM)
+    dma = pltpu.SemaphoreType.DMA
+    return pl.pallas_call(
+        functools.partial(kernel, n_row, n_col, factor),
+        out_shape=(
+            jax.ShapeDtypeStruct((rows, width), jnp.float32),
+            jax.ShapeDtypeStruct((head_rows, head_cols), jnp.float32),
+        ),
+        in_specs=[vmem, vmem, vmem, smem, smem, vmem],
+        out_specs=(vmem, vmem),
+        scratch_shapes=[
+            pltpu.VMEM((rows, width), jnp.bfloat16),
+            pltpu.VMEM((rows, width), jnp.bfloat16),
+            pltpu.VMEM((width, rows), jnp.bfloat16),
+            pltpu.VMEM((head_rows, n_row * rows), jnp.bfloat16),
+            pltpu.VMEM((rows, width), jnp.bfloat16),
+            pltpu.VMEM((rows, masked_width), jnp.bfloat16),
+            pltpu.VMEM((n_row * rows, width), jnp.bfloat16),
+            pltpu.VMEM((head_rows, width), jnp.float32),
+            pltpu.VMEM((head_rows, width), jnp.bfloat16),
+            pltpu.VMEM((n_col - 1, head_rows, window), jnp.bfloat16),
+            dma((2,)),
+            dma((2,)),
+            dma((n_row,)),
+            dma((n_row,)),
+            dma((n_row,)),
+            dma((n_row,)),
+            dma((n_col - 1,)),
+            dma((n_col - 1,)),
+        ],
+        compiler_params=pltpu.CompilerParams(collective_id=0, has_side_effects=True),
+    )(pooled, text_embed, head_weight, logit_scale, logit_bias, partner)
+
+
+def per_device(n_row, n_col):
+    def run(pooled, text_embed, head_weight, logit_scale, logit_bias, partner):
+        rows, width = pooled.shape
+        fused = (
+            n_row % 2 == 0
+            and n_col > 1
+            and rows == LANES
+            and width % LANES == 0
+            and width % (16 * n_row) == 0
+            and width % n_col == 0
+            and window_of(width, n_col)[1]
+        )
+        args = (pooled, text_embed, head_weight, logit_scale, logit_bias, partner)
+        return fused_body(n_row, n_col, *args) if fused else body(*args)
+
+    return run
+
+
 def solution(mesh):
     in_specs = (
         P(("row", "col"), None),
@@ -102,4 +489,5 @@
         P(("row", "col"), None),
     )
     out_specs = (P(("row", "col"), None), P("row", "col"))
-    return jax.shard_map(body, mesh=mesh, in_specs=in_specs, out_specs=out_specs, check_vma=False)
+    run = per_device(mesh.shape["row"], mesh.shape["col"])
+    return jax.shard_map(run, mesh=mesh, in_specs=in_specs, out_specs=out_specs, check_vma=False)

time: 101 us -> 49.8 us (0.49)
  Pallas kernels: 0 us -> 45.4 us
  waiting for transfers between devices: 44.3 us -> 0 us
  matrix products: 22.5 us -> 0 us
  between operations: 16.9 us -> 0.64 us
  starting transfers between devices: 8.91 us -> 0 us
  local copies, waits for them, and re-layouts: 6.56 us -> 3.55 us
    pallas_call x0 -> x1, Pallas kernels: none -> 45.4 us  [fused_body(): pl.pallas_call(functools.partial(kernel, n_row, n_col, factor), out_shape...]
    unnamed x3 -> x0, waiting for transfers between devices: 29.9 us -> none
    dot_general x26 -> x0, matrix products: 22.5 us -> none  [the longest x8 12.2 us: segment_weights(): jnp.dot(image_part[:, low_end:high_end], text_part[:, low_end:high_end].T...]
    all_to_all x1 -> x0, waiting for transfers between devices: 10.8 us -> none  [body(): lax.all_to_all(image_grad.astype(jnp.bfloat16), 'col', split_axis=1, conc...]
    all_to_all x1 -> x0, starting transfers between devices: 6.35 us -> none  [body(): lax.all_to_all(image_grad.astype(jnp.bfloat16), 'col', split_axis=1, conc...]
    ppermute x2 -> x0, waiting for transfers between devices: 3.68 us -> none  [shifted(): lax.ppermute(value, axis, [(i, (i + by) % count) for i in range(count)])]
    ppermute x2 -> x0, starting transfers between devices: 2.52 us -> none  [shifted(): lax.ppermute(value, axis, [(i, (i + by) % count) for i in range(count)])]
    unnamed x32 -> x2, local copies, waits for them, and re-layouts: 5.24 us -> 3.55 us
  transfers between devices with their start and end apart: 5 -> 0, of which waited for: 3 -> 0; matrix products, arithmetic and copies ran while one was open for 23% -> 0% of each run, Pallas kernels for 0% -> 0%
where the time goes in v1:
time: 49.8 us; the launch traced here: 49.6 us
  Pallas kernels  45.4 us (91%)
  local copies, waits for them, and re-layouts  3.55 us (7%)
  between operations  0.64 us (1%)
    pallas_call x1, Pallas kernels, fused_body(): pl.pallas_call(functools.partial(kernel, n_row, n_col, factor), out_shape...  45.4 us
    unnamed x2, local copies, waits for them, and re-layouts  3.55 us

profile of v1, /device:TPU:0, one launch (start us, length us, event | category | flops | bytes accessed | tf_op | source)
XLA Modules:
  0.0 49.6 jit_solution(17798707926154786327)
XLA Ops:
  0.6 45.4 %shard_map.77 = (f32[128,1152]{1,0:T(8,128)}, f32[144,288]{1,0:T(8,128)}) custom-call(bf16[128,1152]{1,0:T(8,128)(2,1)} %pooled_ref.1, bf16[128,1152]{1,0:T(8,128)(2,1)} %text_ref.1, bf16[1152,1152]{1,0:T(8,128)(2,1)} %weight_ref.1, f32[4]{0:T(128)} %scale_ref.1, f32[4]{0:T(128)} %bias_ref.1, s32[1,128]{1,0:T(1,128)} %partner_ref.1), custom_call_target="tpu_custom_call" | custom-call | tf_op jit(solution)/shard_map/pallas_call | solution.py:432
  46.1 1.9 %copy.10 = f32[128,1152]{1,0:T(8,128)} copy(f32[128,1152]{1,0:T(8,128)} %get-tuple-element.4) | data formatting | bytes 1179648
  48.0 1.6 %copy.11 = f32[144,288]{1,0:T(8,128)} copy(f32[144,288]{1,0:T(8,128)} %get-tuple-element.5) | data formatting | bytes 331776

commit v2 on v1

--- a/solution.py
+++ b/solution.py
@@ -155,6 +155,10 @@
     n_row,
     n_col,
     factor,
+    chunks,
+    ready,
+    window,
+    tail_rows,
     pooled_ref,
     text_ref,
     weight_ref,
@@ -186,16 +190,18 @@
     chips = n_row // 2
     head_rows = width // n_row
     head_cols = width // n_col
-    window = landed.shape[2]
     bounds = [0, width // 8, width // 4, width // 2, width]
     row = lax.axis_index("row")
     col = lax.axis_index("col")
     chip = row // 2
     core = row % 2
 
+    side = chip % 2
+    level = chip // 2
+
     def peer(k, e):
-        other = core if e == 0 else 1 - core
-        return ((chip + k) % chips) * 2 + other
+        there = chip + (k % 2) * (1 - 2 * side) + (k // 2) * (2 - 4 * level)
+        return there * 2 + (core if e == 0 else 1 - core)
 
     barrier = pltpu.get_barrier_semaphore()
     for d in range(1, n_row):
@@ -229,7 +235,6 @@
     )
     pl.semaphore_wait(barrier, n_row + n_col - 2)
     behind_copy.start()
-    ahead_copy.start()
 
     for tile in range(width // LANES):
         lanes = pl.ds(tile * LANES, LANES)
@@ -248,7 +253,6 @@
                 pool_recv.at[slot],
                 (target, col),
             )
-            copy.start()
             pool_copies.append(copy)
     pooled_cols[:, pl.ds(0, rows)] = pooled_t[
         pl.ds(pl.multiple_of(row * head_rows, 16), head_rows), :
@@ -287,6 +291,8 @@
         return ref[:, pl.ds(start, stop - start)]
 
     fill_embed(pooled_ref)
+    for copy in pool_copies:
+        copy.start()
     text_id = lax.broadcasted_iota(jnp.int32, (rows, rows), 0)
     positive = (text_id == partner_ref[...]).astype(jnp.float32).T
     own = weights_of(
@@ -297,6 +303,7 @@
         factor,
     )
     behind_copy.wait_recv()
+    ahead_copy.start()
     cross = weights_of(
         lambda q: dot_nt(masked_part(q), text_part(text_behind, q)),
         None,
@@ -314,19 +321,49 @@
 
     by_tile(image_piece, bounds, store_image)
 
-    def slot_rows(slot):
-        return image.at[pl.ds(slot * rows, rows), :]
+    chunk = width // chunks
+    half = rows // 2
+    flip = (2 * col >= n_col).astype(jnp.int32)
+
+    def mirrored(index, count):
+        return flip * index + (1 - flip) * (count - 1 - index)
+
+    def piece_of(slot, i, first=0, count=rows):
+        lanes = pl.ds(pl.multiple_of(mirrored(i, chunks) * chunk, LANES), chunk)
+        return image.at[pl.ds(slot * rows + first, count), lanes]
 
     image_copies = {}
-    for slot in [1] + [2 * k for k in range(1, chips)]:
-        image_copies[slot] = remote(
-            slot_rows(0),
-            slot_rows(slot),
-            image_send.at[slot],
-            image_recv.at[slot],
-            (peer(slot // 2, slot % 2), col),
-        )
-        image_copies[slot].start()
+
+    def send_image(name, src_slot, dst_slot, i, target, first=0, count=rows):
+        image_copies[name, i] = remote(
+            piece_of(src_slot, i, first, count),
+            piece_of(dst_slot, i, first, count),
+            image_send.at[name, i],
+            image_recv.at[name, i],
+            (target, col),
+        )
+        image_copies[name, i].start()
+
+    def send_own(i):
+        send_image(2, 0, 2, i, peer(1, 0))
+        send_image(4, 0, 4, i, peer(2, 0))
+        send_image(1, 0, 1, i, peer(0, 1))
+
+    def pass_direct(i):
+        image_copies[2, i].wait_recv()
+        send_image(6, 2, 6, i, peer(2, 0), 0, half)
+        send_image(3, 2, 3, i, peer(0, 1))
+        image_copies[4, i].wait_recv()
+        send_image(8, 4, 6, i, peer(1, 0), half, half)
+        send_image(5, 4, 5, i, peer(0, 1))
+
+    def pass_corner(i):
+        image_copies[6, i].wait_recv()
+        image_copies[8, i].wait_recv()
+        send_image(7, 6, 7, i, peer(0, 1))
+
+    for i in range(chunks - 1):
+        send_own(i)
 
     def own_text_piece(q, start, stop):
         return dot_nn(own[q].T, embed[:, pl.ds(start, stop - start)])
@@ -336,8 +373,13 @@
 
     by_tile(own_text_piece, bounds, store_text)
 
+    pass_direct(0)
+    send_own(chunks - 1)
     ahead_copy.wait_recv()
     fill_embed(pooled_ahead)
+    pass_corner(0)
+    for i in range(1, chunks):
+        pass_direct(i)
     ahead = weights_of(
         lambda q: dot_nt(text_part(text_ref, q), masked_part(q)),
         None,
@@ -353,75 +395,133 @@
         lanes = pl.ds(base, LANES)
         text_grad_ref[:, lanes] = text_grad_ref[:, lanes] + value
 
-    by_tile(ahead_piece, bounds, add_text)
-
-    for k in range(1, chips):
-        slot = 2 * k
-        image_copies[slot].wait_recv()
-        image_copies[slot + 1] = remote(
-            slot_rows(slot),
-            slot_rows(slot + 1),
-            image_send.at[slot + 1],
-            image_recv.at[slot + 1],
-            (peer(0, 1), col),
-        )
-        image_copies[slot + 1].start()
+    main = head_cols // LANES * LANES
+    tail = head_cols - main
+    groups = head_rows // tail_rows
+
+    def lanes_of(block):
+        first = block * head_cols // LANES * LANES
+        offset = block * head_cols - first
+        part = total[:, pl.ds(pl.multiple_of(first, LANES), window)]
+        return pltpu.roll(part, (window - offset) % window, 1)
+
+    def packed(block):
+        part = lanes_of(block)
+        parts = [part[:, base : base + LANES] for base in range(0, main, LANES)]
+        if tail:
+            last = part[:, main : main + LANES]
+            lane = lax.broadcasted_iota(jnp.int32, last.shape, 1)
+            last = jnp.where(lane < tail, last, 0.0)
+            joined = last[:tail_rows]
+            for j in range(1, groups):
+                here = last[j * tail_rows : (j + 1) * tail_rows]
+                joined = joined + pltpu.roll(here, j * tail, 1)
+            parts.append(joined)
+        return parts
+
+    def out_copy(block):
+        return remote(
+            sent.at[block],
+            landed.at[col],
+            out_send.at[block],
+            out_recv.at[col],
+            (row, block),
+        )
+
+    def in_copy(block):
+        return remote(
+            sent.at[block],
+            landed.at[block],
+            out_send.at[block],
+            out_recv.at[block],
+            (row, block),
+        )
+
     for copy in pool_copies:
         copy.wait_recv()
-    image_copies[1].wait_recv()
-    for k in range(1, chips):
-        image_copies[2 * k + 1].wait_recv()
-    step = 3 * LANES if width % (3 * LANES) == 0 else LANES
-    for base in range(0, width, step):
-        lanes = pl.ds(base, step)
-        part = dot_nn(pooled_cols[...], image[:, lanes])
-        total[:, lanes] = part
-        sent[:, lanes] = part.astype(jnp.bfloat16)
-
-    def out_copy(d):
-        target = (col + d) % n_col
-        first = pl.multiple_of(target * head_cols // LANES * LANES, LANES)
-        return remote(
-            sent.at[:, pl.ds(first, window)],
-            landed.at[d - 1],
-            out_send.at[d - 1],
-            out_recv.at[d - 1],
-            (row, target),
-        )
-
-    out_copies = [out_copy(d) for d in range(n_col - 1, 0, -1)]
-    for copy in out_copies:
-        copy.start()
-    mine = col * head_cols // LANES * LANES
-    result = total[:, pl.ds(pl.multiple_of(mine, LANES), window)]
-    for d in range(1, n_col):
-        out_copies[n_col - 1 - d].wait_recv()
-        result = result + landed[d - 1].astype(jnp.float32)
-    offset = col * head_cols - mine
-    head_grad_ref[...] = pltpu.roll(result, (window - offset) % window, 1)[:, :head_cols]
+    done = 0
+    for i in range(chunks):
+        if i > 0:
+            pass_corner(i)
+        image_copies[1, i].wait_recv()
+        for slot in (3, 5, 7):
+            image_copies[slot, i].wait_recv()
+        lanes = pl.ds(pl.multiple_of(mirrored(i, chunks) * chunk, LANES), chunk)
+        total[:, lanes] = dot_nn(pooled_cols[...], image[:, lanes])
+        while done < n_col and ready[done] <= (i + 1) * chunk:
+            block = mirrored(done, n_col)
+
+            @pl.when(block != col)
+            def _():
+                at = 0
+                for part in packed(block):
+                    count = part.shape[0]
+                    sent[block, pl.ds(at, count), :] = part.astype(jnp.bfloat16)
+                    at += count
+                out_copy(block).start()
+
+            done += 1
+        if i == 0:
+            by_tile(ahead_piece, bounds, add_text)
+
+    results = packed(col)
+    for d in range(n_col - 1, 0, -1):
+        block = (col + d) % n_col
+        in_copy(block).wait_recv()
+        at = 0
+        for n, part in enumerate(results):
+            count = part.shape[0]
+            got = landed[block, pl.ds(at, count), :]
+            results[n] = part + got.astype(jnp.float32)
+            at += count
+    for n in range(main // LANES):
+        head_grad_ref[:, pl.ds(n * LANES, LANES)] = results[n]
+    if tail:
+        for j in range(groups):
+            here = results[-1]
+            if j > 0:
+                here = pltpu.roll(here, LANES - j * tail, 1)
+            head_grad_ref[pl.ds(j * tail_rows, tail_rows), pl.ds(main, tail)] = here[:, :tail]
 
     behind_copy.wait_send()
     ahead_copy.wait_send()
     for copy in pool_copies:
         copy.wait_send()
-    for slot in sorted(image_copies):
-        image_copies[slot].wait_send()
-    for copy in out_copies:
-        copy.wait_send()
-
-
-def window_of(width, n_col):
-    head_cols = width // n_col
+    for name in sorted(image_copies):
+        image_copies[name].wait_send()
+    for d in range(1, n_col):
+        in_copy((col + d) % n_col).wait_send()
+
+
+def plan_of(width, n_row, n_col):
+    head_rows, head_cols = width // n_row, width // n_col
+    chunks = next((n for n in (3, 2, 1) if width % (n * LANES) == 0), None)
     spans = [aligned(c * head_cols, (c + 1) * head_cols) for c in range(n_col)]
     window = max(stop - start for start, stop in spans)
-    fits = all(start + window <= width for start, _ in spans)
-    return window, fits
+    starts = [start for start, _ in spans]
+    if chunks is None or any(start + window > width for start in starts):
+        return None
+    ready = [
+        max(starts[c] + window, width - starts[n_col - 1 - c]) for c in range(n_col)
+    ]
+    tail = head_cols % LANES
+    fitting = [
+        n
+        for n in range(1, LANES // tail + 1 if tail else 2)
+        if head_rows % (16 * n) == 0
+    ]
+    if not fitting or head_cols < LANES:
+        return None
+    return chunks, ready, window, head_rows // max(fitting)
 
 
 def fused_body(n_row, n_col, pooled, text_embed, head_weight, logit_scale, logit_bias, partner):
     rows, width = pooled.shape
     factor = 1.0 / math.sqrt(rows * n_row * n_col)
-    window, _ = window_of(width, n_col)
+    chunks, ready, window, tail_rows = plan_of(width, n_row, n_col)
+    head_cols = width // n_col
+    packed_rows = head_cols // LANES * (width // n_row)
+    packed_rows += tail_rows if head_cols % LANES else 0
     bounds = [0, width // 8, width // 4, width // 2, width]
     spans = [aligned(bounds[q], bounds[q + 1]) for q in range(4)]
     masked_width = sum(stop - start for start, stop in spans)
@@ -430,7 +530,9 @@
     smem = pl.BlockSpec(memory_space=pltpu.SMEM)
     dma = pltpu.SemaphoreType.DMA
     return pl.pallas_call(
-        functools.partial(kernel, n_row, n_col, factor),
+        functools.partial(
+            kernel, n_row, n_col, factor, chunks, ready, window, tail_rows
+        ),
         out_shape=(
             jax.ShapeDtypeStruct((rows, width), jnp.float32),
             jax.ShapeDtypeStruct((head_rows, head_cols), jnp.float32),
@@ -446,16 +548,16 @@
             pltpu.VMEM((rows, masked_width), jnp.bfloat16),
             pltpu.VMEM((n_row * rows, width), jnp.bfloat16),
             pltpu.VMEM((head_rows, width), jnp.float32),
-            pltpu.VMEM((head_rows, width), jnp.bfloat16),
-            pltpu.VMEM((n_col - 1, head_rows, window), jnp.bfloat16),
+            pltpu.VMEM((n_col, packed_rows, LANES), jnp.bfloat16),
+            pltpu.VMEM((n_col, packed_rows, LANES), jnp.bfloat16),
             dma((2,)),
             dma((2,)),
             dma((n_row,)),
             dma((n_row,)),
-            dma((n_row,)),
-            dma((n_row,)),
-            dma((n_col - 1,)),
-            dma((n_col - 1,)),
+            dma((n_row + 1, chunks)),
+            dma((n_row + 1, chunks)),
+            dma((n_col,)),
+            dma((n_col,)),
         ],
         compiler_params=pltpu.CompilerParams(collective_id=0, has_side_effects=True),
     )(pooled, text_embed, head_weight, logit_scale, logit_bias, partner)
@@ -465,13 +567,13 @@
     def run(pooled, text_embed, head_weight, logit_scale, logit_bias, partner):
         rows, width = pooled.shape
         fused = (
-            n_row % 2 == 0
+            n_row == 2**3
             and n_col > 1
             and rows == LANES
             and width % LANES == 0
             and width % (16 * n_row) == 0
             and width % n_col == 0
-            and window_of(width, n_col)[1]
+            and plan_of(width, n_row, n_col) is not None
         )
         args = (pooled, text_embed, head_weight, logit_scale, logit_bias, partner)
         return fused_body(n_row, n_col, *args) if fused else body(*args)

time: 49.8 us -> 42.9 us (0.86)
  Pallas kernels: 45.4 us -> 38.5 us
    pallas_call x1, Pallas kernels: 45.4 us -> 38.5 us  [fused_body(): pl.pallas_call(functools.partial(kernel, n_row, n_col, factor, chunks, re...]
where the time goes in v2:
time: 42.9 us; the launch traced here: 42.7 us
  Pallas kernels  38.5 us (90%)
  local copies, waits for them, and re-layouts  3.55 us (8%)
  between operations  0.64 us (1%)
    pallas_call x1, Pallas kernels, fused_body(): pl.pallas_call(functools.partial(kernel, n_row, n_col, factor, chunks, re...  38.5 us
    unnamed x2, local copies, waits for them, and re-layouts  3.55 us

profile of v2, /device:TPU:0, one launch (start us, length us, event | category | flops | bytes accessed | tf_op | source)
XLA Modules:
  0.0 42.7 jit_solution(11905176954914787308)
XLA Ops:
  0.6 38.5 %shard_map.77 = (f32[128,1152]{1,0:T(8,128)}, f32[144,288]{1,0:T(8,128)}) custom-call(bf16[128,1152]{1,0:T(8,128)(2,1)} %pooled_ref.1, bf16[128,1152]{1,0:T(8,128)(2,1)} %text_ref.1, bf16[1152,1152]{1,0:T(8,128)(2,1)} %weight_ref.1, f32[4]{0:T(128)} %scale_ref.1, f32[4]{0:T(128)} %bias_ref.1, s32[1,128]{1,0:T(1,128)} %partner_ref.1), custom_call_target="tpu_custom_call" | custom-call | tf_op jit(solution)/shard_map/pallas_call | solution.py:532
  39.1 1.9 %copy.10 = f32[128,1152]{1,0:T(8,128)} copy(f32[128,1152]{1,0:T(8,128)} %get-tuple-element.4) | data formatting | bytes 1179648
  41.0 1.6 %copy.11 = f32[144,288]{1,0:T(8,128)} copy(f32[144,288]{1,0:T(8,128)} %get-tuple-element.5) | data formatting | bytes 331776

commit v3 on v2

--- a/solution.py
+++ b/solution.py
@@ -161,12 +161,15 @@
     tail_rows,
     pooled_ref,
     text_ref,
-    weight_ref,
+    weight_hbm,
     scale_ref,
     bias_ref,
     partner_ref,
     text_grad_ref,
     head_grad_ref,
+    weight_ref,
+    weight_sem,
+    image_own,
     pooled_ahead,
     text_behind,
     pooled_t,
@@ -203,6 +206,9 @@
         there = chip + (k % 2) * (1 - 2 * side) + (k // 2) * (2 - 4 * level)
         return there * 2 + (core if e == 0 else 1 - core)
 
+    weight_copy = pltpu.make_async_copy(weight_hbm, weight_ref, weight_sem)
+    weight_copy.start()
+
     barrier = pltpu.get_barrier_semaphore()
     for d in range(1, n_row):
         pl.semaphore_signal(
@@ -290,6 +296,7 @@
         start, stop = aligned(bounds[q], bounds[q + 1])
         return ref[:, pl.ds(start, stop - start)]
 
+    weight_copy.wait()
     fill_embed(pooled_ref)
     for copy in pool_copies:
         copy.start()
@@ -302,8 +309,24 @@
         bias_ref,
         factor,
     )
+
+    def own_image_piece(q, start, stop):
+        return dot_nn(own[q], text_ref[:, pl.ds(start, stop - start)])
+
+    def keep_image(base, value):
+        image_own[:, pl.ds(base, LANES)] = value
+
+    by_tile(own_image_piece, bounds, keep_image)
+
+    def own_text_piece(q, start, stop):
+        return dot_nn(own[q].T, embed[:, pl.ds(start, stop - start)])
+
+    def store_text(base, value):
+        text_grad_ref[:, pl.ds(base, LANES)] = value
+
+    by_tile(own_text_piece, bounds, store_text)
+
     behind_copy.wait_recv()
-    ahead_copy.start()
     cross = weights_of(
         lambda q: dot_nt(masked_part(q), text_part(text_behind, q)),
         None,
@@ -314,10 +337,11 @@
 
     def image_piece(q, start, stop):
         lanes = pl.ds(start, stop - start)
-        return dot_nn(own[q], text_ref[:, lanes]) + dot_nn(cross[q], text_behind[:, lanes])
+        return dot_nn(cross[q], text_behind[:, lanes])
 
     def store_image(base, value):
-        image[pl.ds(0, rows), pl.ds(base, LANES)] = value.astype(jnp.bfloat16)
+        lanes = pl.ds(base, LANES)
+        image[pl.ds(0, rows), lanes] = (image_own[:, lanes] + value).astype(jnp.bfloat16)
 
     by_tile(image_piece, bounds, store_image)
 
@@ -365,35 +389,14 @@
     for i in range(chunks - 1):
         send_own(i)
 
-    def own_text_piece(q, start, stop):
-        return dot_nn(own[q].T, embed[:, pl.ds(start, stop - start)])
-
-    def store_text(base, value):
-        text_grad_ref[:, pl.ds(base, LANES)] = value
-
-    by_tile(own_text_piece, bounds, store_text)
-
     pass_direct(0)
     send_own(chunks - 1)
-    ahead_copy.wait_recv()
-    fill_embed(pooled_ahead)
     pass_corner(0)
+    ahead_copy.start()
     for i in range(1, chunks):
         pass_direct(i)
-    ahead = weights_of(
-        lambda q: dot_nt(text_part(text_ref, q), masked_part(q)),
-        None,
-        scale_ref,
-        bias_ref,
-        factor,
-    )
-
-    def ahead_piece(q, start, stop):
-        return dot_nn(ahead[q], embed[:, pl.ds(start, stop - start)])
-
-    def add_text(base, value):
-        lanes = pl.ds(base, LANES)
-        text_grad_ref[:, lanes] = text_grad_ref[:, lanes] + value
+    for i in range(1, chunks - 1):
+        pass_corner(i)
 
     main = head_cols // LANES * LANES
     tail = head_cols - main
@@ -441,7 +444,7 @@
         copy.wait_recv()
     done = 0
     for i in range(chunks):
-        if i > 0:
+        if i == chunks - 1:
             pass_corner(i)
         image_copies[1, i].wait_recv()
         for slot in (3, 5, 7):
@@ -461,8 +464,25 @@
                 out_copy(block).start()
 
             done += 1
-        if i == 0:
-            by_tile(ahead_piece, bounds, add_text)
+
+    ahead_copy.wait_recv()
+    fill_embed(pooled_ahead)
+    ahead = weights_of(
+        lambda q: dot_nt(text_part(text_ref, q), masked_part(q)),
+        None,
+        scale_ref,
+        bias_ref,
+        factor,
+    )
+
+    def ahead_piece(q, start, stop):
+        return dot_nn(ahead[q], embed[:, pl.ds(start, stop - start)])
+
+    def add_text(base, value):
+        lanes = pl.ds(base, LANES)
+        text_grad_ref[:, lanes] = text_grad_ref[:, lanes] + value
+
+    by_tile(ahead_piece, bounds, add_text)
 
     results = packed(col)
     for d in range(n_col - 1, 0, -1):
@@ -491,6 +511,54 @@
         image_copies[name].wait_send()
     for d in range(1, n_col):
         in_copy((col + d) % n_col).wait_send()
+
+
+def deliver(text_grad, head_grad):
+    parts = 4
+    step = text_grad.shape[0] // parts
+
+    def move(text_from, head_from, text_to, head_to, text_held, head_held, sems, head_sems):
+        def rows_of(ref, n):
+            return ref.at[pl.ds(n * step, step), :]
+
+        loads = [
+            pltpu.make_async_copy(rows_of(text_from, n), rows_of(text_held, n), sems.at[0, n])
+            for n in range(parts)
+        ]
+        head_load = pltpu.make_async_copy(head_from, head_held, head_sems.at[0])
+        for load in loads:
+            load.start()
+        head_load.start()
+        stores = []
+        for n in range(parts):
+            loads[n].wait()
+            stores.append(
+                pltpu.make_async_copy(rows_of(text_held, n), rows_of(text_to, n), sems.at[1, n])
+            )
+            stores[n].start()
+        head_load.wait()
+        head_store = pltpu.make_async_copy(head_held, head_to, head_sems.at[1])
+        head_store.start()
+        for store in stores:
+            store.wait()
+        head_store.wait()
+
+    anywhere = pl.BlockSpec(memory_space=pl.ANY)
+    return pl.pallas_call(
+        move,
+        out_shape=(
+            jax.ShapeDtypeStruct(text_grad.shape, text_grad.dtype),
+            jax.ShapeDtypeStruct(head_grad.shape, head_grad.dtype),
+        ),
+        in_specs=[anywhere, anywhere],
+        out_specs=(anywhere, anywhere),
+        scratch_shapes=[
+            pltpu.VMEM(text_grad.shape, text_grad.dtype),
+            pltpu.VMEM(head_grad.shape, head_grad.dtype),
+            pltpu.SemaphoreType.DMA((2, parts)),
+            pltpu.SemaphoreType.DMA((2,)),
+        ],
+    )(text_grad, head_grad)
 
 
 def plan_of(width, n_row, n_col):
@@ -537,9 +605,12 @@
             jax.ShapeDtypeStruct((rows, width), jnp.float32),
             jax.ShapeDtypeStruct((head_rows, head_cols), jnp.float32),
         ),
-        in_specs=[vmem, vmem, vmem, smem, smem, vmem],
+        in_specs=[vmem, vmem, pl.BlockSpec(memory_space=pl.ANY), smem, smem, vmem],
         out_specs=(vmem, vmem),
         scratch_shapes=[
+            pltpu.VMEM(head_weight.shape, jnp.bfloat16),
+            dma,
+            pltpu.VMEM((rows, width), jnp.float32),
             pltpu.VMEM((rows, width), jnp.bfloat16),
             pltpu.VMEM((rows, width), jnp.bfloat16),
             pltpu.VMEM((width, rows), jnp.bfloat16),
@@ -576,7 +647,7 @@
             and plan_of(width, n_row, n_col) is not None
         )
         args = (pooled, text_embed, head_weight, logit_scale, logit_bias, partner)
-        return fused_body(n_row, n_col, *args) if fused else body(*args)
+        return deliver(*fused_body(n_row, n_col, *args)) if fused else body(*args)
 
     return run
 

time: 42.9 us -> 39.9 us (0.930)
  local copies, waits for them, and re-layouts: 3.55 us -> 0 us
  Pallas kernels: 38.5 us -> 39.1 us
    unnamed x2 -> x0, local copies, waits for them, and re-layouts: 3.55 us -> none
    pallas_call x0 -> x1, Pallas kernels: none -> 2 us  [deliver(): pl.pallas_call(move, out_shape=(jax.ShapeDtypeStruct(text_grad.shape, tex...]
    pallas_call x1, Pallas kernels: 38.5 us -> 37.1 us  [fused_body(): pl.pallas_call(functools.partial(kernel, n_row, n_col, factor, chunks, re...]
where the time goes in v3:
time: 39.9 us; the launch traced here: 39.7 us
  Pallas kernels  39.1 us (98%)
  between operations  0.64 us (2%)
    pallas_call x1, Pallas kernels, fused_body(): pl.pallas_call(functools.partial(kernel, n_row, n_col, factor, chunks, re...  37.1 us
    pallas_call x1, Pallas kernels, deliver(): pl.pallas_call(move, out_shape=(jax.ShapeDtypeStruct(text_grad.shape, tex...  2 us

profile of v3, /device:TPU:0, one launch (start us, length us, event | category | flops | bytes accessed | tf_op | source)
XLA Modules:
  0.0 39.7 jit_solution(8108147937468195849)
XLA Ops:
  0.6 37.1 %shard_map.77 = (f32[128,1152]{1,0:T(8,128)}, f32[144,288]{1,0:T(8,128)}) custom-call(bf16[128,1152]{1,0:T(8,128)(2,1)} %pooled_ref.1, bf16[128,1152]{1,0:T(8,128)(2,1)} %text_ref.1, bf16[1152,1152]{1,0:T(8,128)(2,1)} %weight_hbm.1, f32[4]{0:T(128)} %scale_ref.1, f32[4]{0:T(128)} %bias_ref.1, s32[1,128]{1,0:T(1,128)} %partner_ref.1), custom_call_target="tpu_custom_call" | custom-call | tf_op jit(solution)/shard_map/pallas_call | solution.py:600
  37.7 2.0 %shard_map.78 = (f32[128,1152]{1,0:T(8,128)}, f32[144,288]{1,0:T(8,128)}) custom-call(f32[128,1152]{1,0:T(8,128)} %get-tuple-element.4.text_from, f32[144,288]{1,0:T(8,128)} %get-tuple-element.5.head_from), custom_call_target="tpu_custom_call" | custom-call | tf_op jit(solution)/shard_map/pallas_call | solution.py:547

commit v4 on v3

--- a/solution.py
+++ b/solution.py
@@ -170,7 +170,8 @@
     weight_ref,
     weight_sem,
     image_own,
-    pooled_ahead,
+    cross_text,
+    text_back,
     text_behind,
     pooled_t,
     pooled_cols,
@@ -232,9 +233,9 @@
     behind_copy = remote(
         text_ref, text_behind, near_send.at[0], near_recv.at[0], ((row + 1) % n_row, col)
     )
-    ahead_copy = remote(
-        pooled_ref,
-        pooled_ahead,
+    back_copy = remote(
+        cross_text,
+        text_back,
         near_send.at[1],
         near_recv.at[1],
         ((row + n_row - 1) % n_row, col),
@@ -389,10 +390,18 @@
     for i in range(chunks - 1):
         send_own(i)
 
+    def cross_text_piece(q, start, stop):
+        return dot_nn(cross[q].T, embed[:, pl.ds(start, stop - start)])
+
+    def store_cross(base, value):
+        cross_text[:, pl.ds(base, LANES)] = value.astype(jnp.bfloat16)
+
+    by_tile(cross_text_piece, bounds, store_cross)
+
     pass_direct(0)
     send_own(chunks - 1)
     pass_corner(0)
-    ahead_copy.start()
+    back_copy.start()
     for i in range(1, chunks):
         pass_direct(i)
     for i in range(1, chunks - 1):
@@ -465,24 +474,8 @@
 
             done += 1
 
-    ahead_copy.wait_recv()
-    fill_embed(pooled_ahead)
-    ahead = weights_of(
-        lambda q: dot_nt(text_part(text_ref, q), masked_part(q)),
-        None,
-        scale_ref,
-        bias_ref,
-        factor,
-    )
-
-    def ahead_piece(q, start, stop):
-        return dot_nn(ahead[q], embed[:, pl.ds(start, stop - start)])
-
-    def add_text(base, value):
-        lanes = pl.ds(base, LANES)
-        text_grad_ref[:, lanes] = text_grad_ref[:, lanes] + value
-
-    by_tile(ahead_piece, bounds, add_text)
+    back_copy.wait_recv()
+    text_grad_ref[...] = text_grad_ref[...] + text_back[...].astype(jnp.float32)
 
     results = packed(col)
     for d in range(n_col - 1, 0, -1):
@@ -504,7 +497,7 @@
             head_grad_ref[pl.ds(j * tail_rows, tail_rows), pl.ds(main, tail)] = here[:, :tail]
 
     behind_copy.wait_send()
-    ahead_copy.wait_send()
+    back_copy.wait_send()
     for copy in pool_copies:
         copy.wait_send()
     for name in sorted(image_copies):
@@ -613,6 +606,7 @@
             pltpu.VMEM((rows, width), jnp.float32),
             pltpu.VMEM((rows, width), jnp.bfloat16),
             pltpu.VMEM((rows, width), jnp.bfloat16),
+            pltpu.VMEM((rows, width), jnp.bfloat16),
             pltpu.VMEM((width, rows), jnp.bfloat16),
             pltpu.VMEM((head_rows, n_row * rows), jnp.bfloat16),
             pltpu.VMEM((rows, width), jnp.bfloat16),

time: 39.9 us -> 39.9 us (level)
  no operation moved by 1% of the time
where the time goes in v4:
time: 39.9 us; the launch traced here: 39.7 us
  Pallas kernels  39.1 us (98%)
  between operations  0.64 us (2%)
    pallas_call x1, Pallas kernels, fused_body(): pl.pallas_call(functools.partial(kernel, n_row, n_col, factor, chunks, re...  37.1 us
    pallas_call x1, Pallas kernels, deliver(): pl.pallas_call(move, out_shape=(jax.ShapeDtypeStruct(text_grad.shape, tex...  2 us

profile of v4, /device:TPU:0, one launch (start us, length us, event | category | flops | bytes accessed | tf_op | source)
XLA Modules:
  0.0 39.7 jit_solution(1638387313895582920)
XLA Ops:
  0.6 37.1 %shard_map.77 = (f32[128,1152]{1,0:T(8,128)}, f32[144,288]{1,0:T(8,128)}) custom-call(bf16[128,1152]{1,0:T(8,128)(2,1)} %pooled_ref.1, bf16[128,1152]{1,0:T(8,128)(2,1)} %text_ref.1, bf16[1152,1152]{1,0:T(8,128)(2,1)} %weight_hbm.1, f32[4]{0:T(128)} %scale_ref.1, f32[4]{0:T(128)} %bias_ref.1, s32[1,128]{1,0:T(1,128)} %partner_ref.1), custom_call_target="tpu_custom_call" | custom-call | tf_op jit(solution)/shard_map/pallas_call | solution.py:593
  37.7 2.0 %shard_map.78 = (f32[128,1152]{1,0:T(8,128)}, f32[144,288]{1,0:T(8,128)}) custom-call(f32[128,1152]{1,0:T(8,128)} %get-tuple-element.4.text_from, f32[144,288]{1,0:T(8,128)} %get-tuple-element.5.head_from), custom_call_target="tpu_custom_call" | custom-call | tf_op jit(solution)/shard_map/pallas_call | solution.py:540

commit v5 on v4

--- a/solution.py
+++ b/solution.py
@@ -297,10 +297,10 @@
         start, stop = aligned(bounds[q], bounds[q + 1])
         return ref[:, pl.ds(start, stop - start)]
 
+    for copy in pool_copies:
+        copy.start()
     weight_copy.wait()
     fill_embed(pooled_ref)
-    for copy in pool_copies:
-        copy.start()
     text_id = lax.broadcasted_iota(jnp.int32, (rows, rows), 0)
     positive = (text_id == partner_ref[...]).astype(jnp.float32).T
     own = weights_of(
@@ -401,11 +401,11 @@
     pass_direct(0)
     send_own(chunks - 1)
     pass_corner(0)
-    back_copy.start()
     for i in range(1, chunks):
         pass_direct(i)
     for i in range(1, chunks - 1):
         pass_corner(i)
+    back_copy.start()
 
     main = head_cols // LANES * LANES
     tail = head_cols - main

time: 39.9 us -> 36.6 us (0.917)
  Pallas kernels: 39.1 us -> 35.8 us
    pallas_call x1, Pallas kernels: 37.1 us -> 33.8 us  [fused_body(): pl.pallas_call(functools.partial(kernel, n_row, n_col, factor, chunks, re...]
where the time goes in v5:
time: 36.6 us; the launch traced here: 36.4 us
  Pallas kernels  35.8 us (98%)
  between operations  0.64 us (2%)
    pallas_call x1, Pallas kernels, fused_body(): pl.pallas_call(functools.partial(kernel, n_row, n_col, factor, chunks, re...  33.8 us
    pallas_call x1, Pallas kernels, deliver(): pl.pallas_call(move, out_shape=(jax.ShapeDtypeStruct(text_grad.shape, tex...  2 us

profile of v5, /device:TPU:0, one launch (start us, length us, event | category | flops | bytes accessed | tf_op | source)
XLA Modules:
  0.0 36.4 jit_solution(14998771768816839862)
XLA Ops:
  0.6 33.8 %shard_map.77 = (f32[128,1152]{1,0:T(8,128)}, f32[144,288]{1,0:T(8,128)}) custom-call(bf16[128,1152]{1,0:T(8,128)(2,1)} %pooled_ref.1, bf16[128,1152]{1,0:T(8,128)(2,1)} %text_ref.1, bf16[1152,1152]{1,0:T(8,128)(2,1)} %weight_hbm.1, f32[4]{0:T(128)} %scale_ref.1, f32[4]{0:T(128)} %bias_ref.1, s32[1,128]{1,0:T(1,128)} %partner_ref.1), custom_call_target="tpu_custom_call" | custom-call | tf_op jit(solution)/shard_map/pallas_call | solution.py:593
  34.4 2.0 %shard_map.78 = (f32[128,1152]{1,0:T(8,128)}, f32[144,288]{1,0:T(8,128)}) custom-call(f32[128,1152]{1,0:T(8,128)} %get-tuple-element.4.text_from, f32[144,288]{1,0:T(8,128)} %get-tuple-element.5.head_from), custom_call_target="tpu_custom_call" | custom-call | tf_op jit(solution)/shard_map/pallas_call | solution.py:540
